TPU v7x, 32 devices: a whole 2x2x4 slice. The times are simulated.
32 devices in a mesh: wide: 8 (over y, x, core), narrow: 4 (over z).
Axes of the slice: x: 2, y: 2, z: 4, core: 2. Of those that a mesh axis runs over, the one named last changes fastest.
Arguments:
- layer_input: bfloat16 [2, 8, 256, 2048], P(None, 'wide', 'narrow'), may hold values from -6 to 6
- document_lengths: int32 [2, 8, 4], P(None, 'wide'), may hold values from 1 to 128, 256 in all within a row
- attn_gain: bfloat16 [2048], replicated, may hold values from 0.5 to 1.5
- w_query: bfloat16 [2048, 2048], P(None, 'narrow'), may hold values from -0.125 to 0.125
- w_key: bfloat16 [2048, 1024], P(None, 'narrow'), may hold values from -0.125 to 0.125
- w_value: bfloat16 [2048, 1024], P(None, 'narrow'), may hold values from -0.125 to 0.125
- query_gain: bfloat16 [128], replicated, may hold values from 1 to 2.5
- key_gain: bfloat16 [128], replicated, may hold values from 1 to 2.5
- w_out: bfloat16 [2048, 2048], P('narrow'), may hold values from -0.75 to 0.75
- mlp_gain: bfloat16 [2048], replicated, may hold values from 0.5 to 1.5
- w_gate: bfloat16 [2048, 6144], P(None, 'narrow'), may hold values from -0.125 to 0.125
- w_up: bfloat16 [2048, 6144], P(None, 'narrow'), may hold values from -0.125 to 0.125
- w_down: bfloat16 [6144, 2048], P('narrow'), may hold values from -0.078125 to 0.078125
- output_cotangent: bfloat16 [2, 8, 256, 2048], P(None, 'wide', 'narrow'), may hold values from -6 to 6
Outputs:
- layer_out: float32 [2, 8, 256, 2048], P(None, 'wide', 'narrow')
- in_grad: float32 [2, 8, 256, 2048], P(None, 'wide', 'narrow')
- attn_gain_grad: float32 [2048], replicated
- w_query_grad: float32 [2048, 2048], P('wide', 'narrow')
- w_key_grad: float32 [2048, 1024], P('wide', 'narrow')
- w_value_grad: float32 [2048, 1024], P('wide', 'narrow')
- query_gain_grad: float32 [128], replicated
- key_gain_grad: float32 [128], replicated
- w_out_grad: float32 [2048, 2048], P('narrow', 'wide')
- mlp_gain_grad: float32 [2048], replicated
- w_gate_grad: float32 [2048, 6144], P('wide', 'narrow')
- w_up_grad: float32 [2048, 6144], P('wide', 'narrow')
- w_down_grad: float32 [6144, 2048], P('narrow', 'wide')
Inputs may be any that keep to these rules, and one draw needn't show every extreme that they name: `document_lengths`: each row's 4 document lengths sum to 256, and in every row the longest is exactly 128.
All inputs are finite; a program needn't handle non-finite values.
Results may differ from a plain program's by a relative error of at most 0.013.
The roundings to bfloat16 on the way count: a program that leaves them out, or rounds other values in their place, can miss the bound.
Values may be sent and summed in bfloat16 or wider, within the bound.
A program may use at most 192 MiB of HBM per device.

v0:
```python
import jax
import jax.numpy as jnp
from jax import lax
from jax.sharding import PartitionSpec as P

norm_eps = 1e-06
masked_score = -1e30


def rms_scale(values):
    return lax.rsqrt(jnp.mean(values * values, axis=-1, keepdims=True) + norm_eps)


def rms_back(grad_in, normed_hat, scale_rows):
    return scale_rows * (
        grad_in - normed_hat * jnp.mean(grad_in * normed_hat, axis=-1, keepdims=True)
    )


def doc_layout(lengths, seq_len):
    doc_ends = jnp.cumsum(lengths)
    starts = doc_ends - lengths
    places = lax.iota(jnp.int32, seq_len)
    segment = jnp.sum((places[:, None] >= doc_ends[None, :]).astype(jnp.int32), axis=1)
    member = segment[:, None] == lax.iota(jnp.int32, lengths.shape[0])[None, :]
    doc_first = jnp.sum(jnp.where(member, starts[None, :], 0), axis=1)
    allowed = (segment[:, None] == segment[None, :]) & (places[None, :] <= places[:, None])
    return (places - doc_first, allowed)


def rope_tables(inside, head_dim):
    half_dim = head_dim // 2
    frequency = jnp.power(1000000.0, -2.0 * lax.iota(jnp.float32, half_dim) / head_dim)
    angles = inside.astype(jnp.float32)[:, None] * frequency[None, :]
    return (jnp.cos(angles), jnp.sin(angles))


def rotate(values, cos_table, sine_table):
    half_dim = values.shape[-1] // 2
    first_half = values[..., :half_dim]
    second = values[..., half_dim:]
    cos_wide = cos_table[:, None, :]
    sine_wide = sine_table[:, None, :]
    return jnp.concatenate(
        [first_half * cos_wide - second * sine_wide, second * cos_wide + first_half * sine_wide],
        axis=-1,
    )


def contract_rows(left_side, right_side):
    return lax.dot_general(
        left_side, right_side, (((0,), (0,)), ((), ())), preferred_element_type=jnp.float32
    )


def contract_cols(left_side, right_side):
    return lax.dot_general(
        left_side, right_side, (((1,), (1,)), ((), ())), preferred_element_type=jnp.float32
    )


def row_product(source, weight):
    return jnp.dot(source, weight, preferred_element_type=jnp.float32)


def row_back_product(source, weight):
    return contract_cols(source, weight)


def attention_scores(grouped, key_rot, allowed, score_scale):
    raw_scores = (
        jnp.einsum("tkgd,ukd->kgtu", grouped, key_rot, preferred_element_type=jnp.float32)
        * score_scale
    )
    return jnp.where(allowed[None, None], raw_scores, masked_score)


def local(
    layer_input,
    document_lengths,
    attn_gain,
    w_query,
    w_key,
    w_value,
    query_gain,
    key_gain,
    w_out,
    mlp_gain,
    w_gate,
    w_up,
    w_down,
    output_cotangent,
):
    shard_rows = layer_input.shape[2]
    seq_len = shard_rows * lax.axis_size("narrow")
    head_dim = query_gain.shape[0]
    query_cols = w_query.shape[1]
    key_cols = w_key.shape[1]
    query_heads = query_cols // head_dim
    kv_local = key_cols // head_dim
    group_size = query_cols // key_cols
    ff_cols = w_gate.shape[1]
    score_scale = head_dim ** (-0.5)
    w_qkv = jnp.concatenate([w_query, w_key, w_value], axis=1)
    w_both = jnp.concatenate([w_gate, w_up], axis=1)
    attn_gain_f = attn_gain.astype(jnp.float32)
    query_gain_f = query_gain.astype(jnp.float32)
    key_gain_f = key_gain.astype(jnp.float32)
    mlp_gain_f = mlp_gain.astype(jnp.float32)
    totals = None
    small_totals = None
    outputs_list = []
    in_grads = []
    for micro_step in range(layer_input.shape[0]):
        rows_in = layer_input[micro_step, 0].astype(jnp.float32)
        inside, allowed = doc_layout(document_lengths[micro_step, 0], seq_len)
        cos_table, sine_table = rope_tables(inside, head_dim)
        scale_one = rms_scale(rows_in)
        hat_one = rows_in * scale_one
        normed = (hat_one * attn_gain_f).astype(jnp.bfloat16)
        normed_full = lax.all_gather(normed, "narrow", axis=0, tiled=True)
        projected = jnp.dot(normed_full, w_qkv, preferred_element_type=jnp.float32)
        query_raw = projected[:, :query_cols].reshape(seq_len, query_heads, head_dim)
        key_raw = projected[:, query_cols : query_cols + key_cols].reshape(
            seq_len, kv_local, head_dim
        )
        value_rows = (
            projected[:, query_cols + key_cols :]
            .astype(jnp.bfloat16)
            .reshape(seq_len, kv_local, head_dim)
        )
        query_scale = rms_scale(query_raw)
        query_hat = query_raw * query_scale
        query_rot = rotate(query_hat * query_gain_f, cos_table, sine_table).astype(jnp.bfloat16)
        key_scale = rms_scale(key_raw)
        key_hat = key_raw * key_scale
        key_rot = rotate(key_hat * key_gain_f, cos_table, sine_table).astype(jnp.bfloat16)
        grouped = query_rot.reshape(seq_len, kv_local, group_size, head_dim)
        scores = attention_scores(grouped, key_rot, allowed, score_scale)
        top_score = jnp.max(scores, axis=-1, keepdims=True)
        exponent = jnp.exp(scores - top_score)
        total_mass = jnp.sum(exponent, axis=-1, keepdims=True)
        log_mass = top_score + jnp.log(total_mass)
        prob_low = (exponent / total_mass).astype(jnp.bfloat16)
        attn_mix = jnp.einsum(
            "kgtu,ukd->tkgd", prob_low, value_rows, preferred_element_type=jnp.float32
        )
        attn_mix = attn_mix.reshape(seq_len, query_cols).astype(jnp.bfloat16)
        attn_branch = lax.psum_scatter(
            row_product(attn_mix, w_out), "narrow", scatter_dimension=0, tiled=True
        )
        middle = rows_in + attn_branch
        scale_two = rms_scale(middle)
        hat_two = middle * scale_two
        normed_two = (hat_two * mlp_gain_f).astype(jnp.bfloat16)
        normed_two_full = lax.all_gather(normed_two, "narrow", axis=0, tiled=True)
        gate_up = jnp.dot(normed_two_full, w_both, preferred_element_type=jnp.float32)
        gate_pre = gate_up[:, :ff_cols]
        up_proj = gate_up[:, ff_cols:]
        sigmoid_gate = jax.nn.sigmoid(gate_pre)
        silu_gate = gate_pre * sigmoid_gate
        activated = (silu_gate * up_proj).astype(jnp.bfloat16)
        mlp_branch = lax.psum_scatter(
            row_product(activated, w_down).astype(jnp.bfloat16),
            "narrow",
            scatter_dimension=0,
            tiled=True,
        ).astype(jnp.float32)
        outputs_list.append(middle + mlp_branch)
        cot_rows = output_cotangent[micro_step, 0]
        cot_full = lax.all_gather(cot_rows, "narrow", axis=0, tiled=True)
        grad_down = contract_rows(activated, cot_full)
        d_act = contract_cols(cot_full, w_down)
        d_gate = d_act * up_proj * sigmoid_gate * (1.0 + gate_pre * (1.0 - sigmoid_gate))
        d_up = d_act * silu_gate
        d_both = jnp.concatenate([d_gate, d_up], axis=1).astype(jnp.bfloat16)
        grad_both = contract_rows(normed_two_full, d_both)
        d_normed_two = lax.psum_scatter(
            row_back_product(d_both, w_both), "narrow", scatter_dimension=0, tiled=True
        )
        mlp_gain_part = jnp.sum(d_normed_two * hat_two, axis=0)
        d_middle = cot_rows.astype(jnp.float32) + rms_back(
            d_normed_two * mlp_gain_f, hat_two, scale_two
        )
        d_branch = d_middle.astype(jnp.bfloat16)
        d_branch_full = lax.all_gather(d_branch, "narrow", axis=0, tiled=True)
        grad_out = contract_rows(attn_mix, d_branch_full)
        d_mix = contract_cols(d_branch_full, w_out).astype(jnp.bfloat16)
        d_mix = d_mix.reshape(seq_len, kv_local, group_size, head_dim)
        d_prob = jnp.einsum("tkgd,ukd->kgtu", d_mix, value_rows, preferred_element_type=jnp.float32)
        scores_again = attention_scores(grouped, key_rot, allowed, score_scale)
        prob_again = jnp.exp(scores_again - log_mass)
        prob_back_low = prob_again.astype(jnp.bfloat16)
        d_value = jnp.einsum(
            "kgtu,tkgd->ukd", prob_back_low, d_mix, preferred_element_type=jnp.float32
        )
        d_score = prob_again * (d_prob - jnp.sum(prob_again * d_prob, axis=-1, keepdims=True))
        d_score = d_score.astype(jnp.bfloat16)
        d_query = jnp.einsum("kgtu,ukd->tkgd", d_score, key_rot, preferred_element_type=jnp.float32)
        d_query = d_query.reshape(seq_len, query_heads, head_dim) * score_scale
        d_key = (
            jnp.einsum("kgtu,tkgd->ukd", d_score, grouped, preferred_element_type=jnp.float32)
            * score_scale
        )
        d_query_norm = rotate(d_query, cos_table, -sine_table)
        d_key_norm = rotate(d_key, cos_table, -sine_table)
        query_gain_part = jnp.sum(d_query_norm * query_hat, axis=(0, 1))
        key_gain_part = jnp.sum(d_key_norm * key_hat, axis=(0, 1))
        d_query_raw = rms_back(d_query_norm * query_gain_f, query_hat, query_scale)
        d_key_raw = rms_back(d_key_norm * key_gain_f, key_hat, key_scale)
        d_proj = jnp.concatenate(
            [
                d_query_raw.reshape(seq_len, query_cols),
                d_key_raw.reshape(seq_len, key_cols),
                d_value.reshape(seq_len, key_cols),
            ],
            axis=1,
        ).astype(jnp.bfloat16)
        grad_qkv = contract_rows(normed_full, d_proj)
        d_normed = lax.psum_scatter(
            row_back_product(d_proj, w_qkv), "narrow", scatter_dimension=0, tiled=True
        )
        attn_gain_part = jnp.sum(d_normed * hat_one, axis=0)
        in_grads.append(d_middle + rms_back(d_normed * attn_gain_f, hat_one, scale_one))
        grads_now = (grad_qkv, grad_both, grad_out, grad_down)
        small_now = (attn_gain_part, query_gain_part, key_gain_part, mlp_gain_part)
        if totals is None:
            totals = grads_now
            small_totals = small_now
        else:
            totals = tuple((running + extra for running, extra in zip(totals, grads_now)))
            small_totals = tuple(
                (running + extra for running, extra in zip(small_totals, small_now))
            )
    totals = (
        lax.psum_scatter(totals[0], "wide", scatter_dimension=0, tiled=True),
        lax.psum_scatter(totals[1], "wide", scatter_dimension=0, tiled=True),
        lax.psum_scatter(totals[2], "wide", scatter_dimension=1, tiled=True),
        lax.psum_scatter(totals[3], "wide", scatter_dimension=1, tiled=True),
    )
    small_sums = lax.psum(small_totals, ("wide", "narrow"))
    qkv_share, both_share, out_share, down_share = totals
    layer_out = jnp.stack(outputs_list)[:, None]
    in_grad = jnp.stack(in_grads)[:, None]
    return (
        layer_out,
        in_grad,
        small_sums[0],
        qkv_share[:, :query_cols],
        qkv_share[:, query_cols : query_cols + key_cols],
        qkv_share[:, query_cols + key_cols :],
        small_sums[1],
        small_sums[2],
        out_share,
        small_sums[3],
        both_share[:, :ff_cols],
        both_share[:, ff_cols:],
        down_share,
    )


def solution(mesh):
    in_specs = (
        P(None, "wide", "narrow", None),
        P(None, "wide", None),
        P(),
        P(None, "narrow"),
        P(None, "narrow"),
        P(None, "narrow"),
        P(),
        P(),
        P("narrow", None),
        P(),
        P(None, "narrow"),
        P(None, "narrow"),
        P("narrow", None),
        P(None, "wide", "narrow", None),
    )
    out_specs = (
        P(None, "wide", "narrow", None),
        P(None, "wide", "narrow", None),
        P(),
        P("wide", "narrow"),
        P("wide", "narrow"),
        P("wide", "narrow"),
        P(),
        P(),
        P("narrow", "wide"),
        P(),
        P("wide", "narrow"),
        P("wide", "narrow"),
        P("narrow", "wide"),
    )
    return jax.shard_map(local, mesh=mesh, in_specs=in_specs, out_specs=out_specs, check_vma=False)
```

profile of v0, /device:TPU:0, one launch (start us, length us, event | category | flops | bytes accessed | tf_op | source)
XLA Modules:
  0.0 1073.6 jit_solution(3452140487380955168)
XLA Ops:
  23.4 18.8 %all-gather.11.cloned.1.call-done = bf16[256,2048]{1,0:T(8,128)(2,1)} async-done(((bf16[64,2048]{1,0:T(8,128)(2,1)}), bf16[256,2048]{1,0:T(8,128)(2,1)}) %all-gather.11.cloned.1.call-update) | async-done | bytes 1048592 | tf_op jit(solution)/shard_map/all_gather | solution.py:121
  47.8 24.1 %all-gather.15.cloned.1.call-done = bf16[256,2048]{1,0:T(8,128)(2,1)} async-done(((bf16[64,2048]{1,0:T(8,128)(2,1)}), bf16[256,2048]{1,0:T(8,128)(2,1)}) %all-gather.15.cloned.1.call-update) | async-done | bytes 1048592 | tf_op jit(solution)/shard_map/all_gather | solution.py:121
  114.8 31.8 %reduce-scatter.13.cloned.1.call-done = f32[64,2048]{1,0:T(8,128)} async-done(((f32[256,2048]{1,0:T(8,128)}), f32[64,2048]{1,0:T(8,128)}) %reduce-scatter.13.cloned.1.call-update) | async-done | bytes 524304 | tf_op jit(solution)/shard_map/reduce_scatter | solution.py:149
  146.6 45.5 %reduce-scatter.17.cloned.1.call-done = f32[64,2048]{1,0:T(8,128)} async-done(((f32[256,2048]{1,0:T(8,128)}), f32[64,2048]{1,0:T(8,128)}) %reduce-scatter.17.cloned.1.call-update) | async-done | bytes 524304 | tf_op jit(solution)/shard_map/reduce_scatter | solution.py:149
  210.8 13.3 %all-gather.13.cloned.1.call-done = bf16[256,2048]{1,0:T(8,128)(2,1)} async-done(((bf16[64,2048]{1,0:T(8,128)(2,1)}), bf16[256,2048]{1,0:T(8,128)(2,1)}) %all-gather.13.cloned.1.call-update) | async-done | bytes 1048592 | tf_op jit(solution)/shard_map/all_gather | solution.py:156
  224.0 10.0 fusion.112
  234.0 19.5 %all-gather.23.cloned.1.call-done = bf16[1,1,256,2048]{3,2,1,0:T(8,128)(2,1)} async-done(((bf16[1,1,64,2048]{3,2,1,0:T(8,128)(2,1)}), bf16[1,1,256,2048]{3,2,1,0:T(8,128)(2,1)}) %all-gather.23.cloned.1.call-update) | async-done | bytes 1048592 | tf_op jit(solution)/shard_map/all_gather | solution.py:171
  272.5 42.3 %reduce-scatter.21.cloned.1.call-done = f32[64,2048]{1,0:T(8,128)} async-done(((f32[256,2048]{1,0:T(8,128)}), f32[64,2048]{1,0:T(8,128)}) %reduce-scatter.21.cloned.1.call-update) | async-done | bytes 524304 | tf_op jit(solution)/shard_map/reduce_scatter | solution.py:178
  318.9 26.2 %all-gather.17.cloned.1.call-done = bf16[256,2048]{1,0:T(8,128)(2,1)} async-done(((bf16[64,2048]{1,0:T(8,128)(2,1)}), bf16[256,2048]{1,0:T(8,128)(2,1)}) %all-gather.17.cloned.1.call-update) | async-done | bytes 1048592 | tf_op jit(solution)/shard_map/all_gather | solution.py:156
  345.1 10.0 fusion.115
  355.1 19.1 %all-gather.25.cloned.1.call-done = bf16[1,1,256,2048]{3,2,1,0:T(8,128)(2,1)} async-done(((bf16[1,1,64,2048]{3,2,1,0:T(8,128)(2,1)}), bf16[1,1,256,2048]{3,2,1,0:T(8,128)(2,1)}) %all-gather.25.cloned.1.call-update) | async-done | bytes 1048592 | tf_op jit(solution)/shard_map/all_gather | solution.py:171
  382.6 9.4 fusion.19
  399.1 36.4 %reduce-scatter.25.cloned.1.call-done = f32[64,2048]{1,0:T(8,128)} async-done(((f32[256,2048]{1,0:T(8,128)}), f32[64,2048]{1,0:T(8,128)}) %reduce-scatter.25.cloned.1.call-update) | async-done | bytes 524304 | tf_op jit(solution)/shard_map/reduce_scatter | solution.py:178
  438.1 26.9 %reduce-scatter.19.cloned.1.call-done = bf16[64,2048]{1,0:T(8,128)(2,1)} async-done(((bf16[256,2048]{1,0:T(8,128)(2,1)}), bf16[64,2048]{1,0:T(8,128)(2,1)}) %reduce-scatter.19.cloned.1.call-update) | async-done | bytes 262160 | tf_op jit(solution)/shard_map/reduce_scatter | solution.py:163
  473.6 21.0 %all-gather.19.cloned.1.call-done = bf16[256,2048]{1,0:T(8,128)(2,1)} async-done(((bf16[64,2048]{1,0:T(8,128)(2,1)}), bf16[256,2048]{1,0:T(8,128)(2,1)}) %all-gather.19.cloned.1.call-update) | async-done | bytes 1048592 | tf_op jit(solution)/shard_map/all_gather | solution.py:186
  504.7 19.0 %all-gather.21.cloned.1.call-done = bf16[256,2048]{1,0:T(8,128)(2,1)} async-done(((bf16[64,2048]{1,0:T(8,128)(2,1)}), bf16[256,2048]{1,0:T(8,128)(2,1)}) %all-gather.21.cloned.1.call-update) | async-done | bytes 1048592 | tf_op jit(solution)/shard_map/all_gather | solution.py:186
  589.7 11.6 %fusion.20 = f32[2048,3072]{1,0:T(8,128)} fusion(bf16[256,2048]{1,0:T(8,128)(2,1)S(1)} %copy-done.44, bf16[256,1536]{1,0:T(8,128)(2,1)} %copy-done.67, bf16[256,1536]{1,0:T(8,128)(2,1)} %copy-done.66), kind=kOutput, calls=%fused_computation.62 | convolution fusion | flops 3224371200 | bytes 27787264 | tf_op jit(solution)/shard_map/dot_general | solution.py:51
  601.3 16.9 %convolution_add_fusion = f32[2048,3072]{1,0:T(8,128)} fusion(f32[2048,3072]{1,0:T(8,128)} %fusion.20, bf16[256,2048]{1,0:T(8,128)(2,1)S(1)} %copy-done.40, bf16[256,1536]{1,0:T(8,128)(2,1)} %copy-done.64, bf16[256,1536]{1,0:T(8,128)(2,1)S(1)} %copy-done.63), kind=kOutput, calls=%fused_computation | convolution fusion | flops 3230662656 | bytes 52953088 | tf_op jit(solution)/shard_map/dot_general | solution.py:51
  634.6 15.6 %reduce-scatter.27.cloned.1.call-done = f32[64,2048]{1,0:T(8,128)} async-done(((f32[256,2048]{1,0:T(8,128)}), f32[64,2048]{1,0:T(8,128)}) %reduce-scatter.27.cloned.1.call-update) | async-done | bytes 524304 | tf_op jit(solution)/shard_map/reduce_scatter | solution.py:220
  651.9 41.1 %all-reduce = (f32[2048]{0:T(1024)}, f32[128]{0:T(128)}, f32[128]{0:T(128)}, f32[2048]{0:T(1024)}) all-reduce(f32[2048]{0:T(1024)S(1)} %add.226, f32[128]{0:T(128)S(1)} %add.228, f32[128]{0:T(128)S(1)} %add.229, f32[2048]{0:T(1024)S(1)} %add.231), channel_id=1, replica_groups=mesh['wide'=8,'narrow'=4] {'wide','narrow'}, use_global_device_ids=true, to_apply=%region_38.39 | all-reduce | flops 4352 | bytes 34816 | tf_op jit(solution)/shard_map/psum | solution.py:241
  697.4 56.1 %reduce-scatter.29.cloned.1.call-done = f32[256,1024]{1,0:T(8,128)} async-done(((f32[2048,1024]{1,0:T(8,128)}), f32[256,1024]{1,0:T(8,128)}) %reduce-scatter.29.cloned.1.call-update) | async-done | bytes 1048592 | tf_op jit(solution)/shard_map/reduce_scatter | solution.py:236
  757.4 157.0 %reduce-scatter.33.cloned.1.call-done = f32[256,3072]{1,0:T(8,128)} async-done(((f32[2048,3072]{1,0:T(8,128)}), f32[256,3072]{1,0:T(8,128)}) %reduce-scatter.33.cloned.1.call-update) | async-done | bytes 3145744 | tf_op jit(solution)/shard_map/reduce_scatter | solution.py:237
  918.1 51.9 %reduce-scatter.31.cloned.1.call-done = f32[512,256]{1,0:T(8,128)} async-done(((f32[512,2048]{1,0:T(8,128)}), f32[512,256]{1,0:T(8,128)}) %reduce-scatter.31.cloned.1.call-update) | async-done | bytes 524304 | tf_op jit(solution)/shard_map/reduce_scatter | solution.py:238
  970.0 96.3 %reduce-scatter.35.cloned.1.call-done = f32[1536,256]{1,0:T(8,128)} async-done(((f32[1536,2048]{1,0:T(8,128)}), f32[1536,256]{1,0:T(8,128)}) %reduce-scatter.35.cloned.1.call-update) | async-done | bytes 1572880 | tf_op jit(solution)/shard_map/reduce_scatter | solution.py:239
  (410 shorter events, 237.8 us)
Async XLA Ops:
  7.2 93.8 %copy-start = (bf16[512,2048]{1,0:T(8,128)(2,1)S(1)}, bf16[512,2048]{1,0:T(8,128)(2,1)}, u32[]{:S(2)}) copy-start(bf16[512,2048]{1,0:T(8,128)(2,1)} %param.22) | copy-start | bytes 6291460
  7.2 35.1 %all-gather.11.cloned.1.call-start = ((), (), s32[]{:S(2)}) async-start(), calls=%async_computation.12 | async-start | bytes 1310720 | tf_op jit(solution)/shard_map/all_gather | solution.py:121
  11.5 60.4 %all-gather.15.cloned.1.call-start = ((), (), s32[]{:S(2)}) async-start(), calls=%async_computation.16 | async-start | bytes 1310720 | tf_op jit(solution)/shard_map/all_gather | solution.py:121
  12.2 134.4 %reduce-scatter.13.cloned.1.call-start = ((), (), s32[]{:S(2)}) async-start(), calls=%async_computation.13 | async-start | bytes 2621440 | tf_op jit(solution)/shard_map/reduce_scatter | solution.py:149
  15.6 76.6 %copy-start.102 = (f32[128]{0:T(128)}, f32[128]{0:T(128)S(1)}, u32[]{:S(2)}) copy-start(f32[128]{0:T(128)S(1)} %convert_element_type.145) | copy-start | bytes 1540
  90.6 380.7 %copy-start.83 = (f32[256,2]{0,1:T(2,128)}, f32[256,2]{0,1:T(2,128)S(1)}, u32[]{:S(2)}) copy-start(f32[256,2]{0,1:T(2,128)S(1)} %add_rsqrt_fusion.3) | copy-start | bytes 6148
  103.1 89.0 %reduce-scatter.17.cloned.1.call-start = ((), (), s32[]{:S(2)}) async-start(), calls=%async_computation.17 | async-start | bytes 2621440 | tf_op jit(solution)/shard_map/reduce_scatter | solution.py:149
  114.1 110.0 %all-gather.13.cloned.1.call-start = ((), (), s32[]{:S(2)}) async-start(), calls=%async_computation.14 | async-start | bytes 1310720 | tf_op jit(solution)/shard_map/all_gather | solution.py:156
  196.6 56.9 %all-gather.23.cloned.1.call-start = ((), (), s32[]{:S(2)}) async-start(), calls=%async_computation.30 | async-start | bytes 1310720 | tf_op jit(solution)/shard_map/all_gather | solution.py:171
  198.6 116.2 %reduce-scatter.21.cloned.1.call-start = ((), (), s32[]{:S(2)}) async-start(), calls=%async_computation.20 | async-start | bytes 2621440 | tf_op jit(solution)/shard_map/reduce_scatter | solution.py:178
  271.2 73.9 %all-gather.17.cloned.1.call-start = ((), (), s32[]{:S(2)}) async-start(), calls=%async_computation.18 | async-start | bytes 1310720 | tf_op jit(solution)/shard_map/all_gather | solution.py:156
  317.7 56.5 %all-gather.25.cloned.1.call-start = ((), (), s32[]{:S(2)}) async-start(), calls=%async_computation.31 | async-start | bytes 1310720 | tf_op jit(solution)/shard_map/all_gather | solution.py:171
  318.4 117.1 %reduce-scatter.25.cloned.1.call-start = ((), (), s32[]{:S(2)}) async-start(), calls=%async_computation.23 | async-start | bytes 2621440 | tf_op jit(solution)/shard_map/reduce_scatter | solution.py:178
  392.0 72.9 %reduce-scatter.19.cloned.1.call-start = ((), (), s32[]{:S(2)}) async-start(), calls=%async_computation.19 | async-start | bytes 1310720 | tf_op jit(solution)/shard_map/reduce_scatter | solution.py:163
  397.9 96.7 %all-gather.19.cloned.1.call-start = ((), (), s32[]{:S(2)}) async-start(), calls=%async_computation.21 | async-start | bytes 1310720 | tf_op jit(solution)/shard_map/all_gather | solution.py:186
  467.9 55.8 %all-gather.21.cloned.1.call-start = ((), (), s32[]{:S(2)}) async-start(), calls=%async_computation.24 | async-start | bytes 1310720 | tf_op jit(solution)/shard_map/all_gather | solution.py:186
  468.6 166.0 %reduce-scatter.23.cloned.1.call-start = ((), (), s32[]{:S(2)}) async-start(), calls=%async_computation.22 | async-start | bytes 2621440 | tf_op jit(solution)/shard_map/reduce_scatter | solution.py:220
  561.3 88.9 %reduce-scatter.27.cloned.1.call-start = ((), (), s32[]{:S(2)}) async-start(), calls=%async_computation.25 | async-start | bytes 2621440 | tf_op jit(solution)/shard_map/reduce_scatter | solution.py:220
  575.7 117.3 %reduce-scatter.15.cloned.1.call-start = ((), (), s32[]{:S(2)}) async-start(), calls=%async_computation.15 | async-start | bytes 1310720 | tf_op jit(solution)/shard_map/reduce_scatter | solution.py:163
  581.5 172.0 %reduce-scatter.29.cloned.1.call-start = ((), (), s32[]{:S(2)}) async-start(), calls=%async_computation.26 | async-start | bytes 9437184 | tf_op jit(solution)/shard_map/reduce_scatter | solution.py:236
  588.5 325.8 %reduce-scatter.33.cloned.1.call-start = ((), (), s32[]{:S(2)}) async-start(), calls=%async_computation.28 | async-start | bytes 28311552 | tf_op jit(solution)/shard_map/reduce_scatter | solution.py:237
  618.3 351.7 %reduce-scatter.31.cloned.1.call-start = ((), (), s32[]{:S(2)}) async-start(), calls=%async_computation.27 | async-start | bytes 4718592 | tf_op jit(solution)/shard_map/reduce_scatter | solution.py:238
  623.1 443.2 %reduce-scatter.35.cloned.1.call-start = ((), (), s32[]{:S(2)}) async-start(), calls=%async_computation.29 | async-start | bytes 14155776 | tf_op jit(solution)/shard_map/reduce_scatter | solution.py:239
  755.4 311.0 %copy-start.1 = (bf16[512,2048]{1,0:T(8,128)(2,1)S(1)}, bf16[512,2048]{1,0:T(8,128)(2,1)}, u32[]{:S(2)}) copy-start(bf16[512,2048]{1,0:T(8,128)(2,1)} %param.22) | copy-start | bytes 6291460
  (100 other events, 965.5 us)
Sparse Core Ops, SparseCore 0:
  11.6 30.6 all-gather.10
  44.4 27.4 all-gather.14
  103.2 43.3 reduce-scatter.12
  148.8 43.1 reduce-scatter.16
  196.8 27.2 all-gather.12
  226.0 27.4 all-gather.22
  271.4 43.3 reduce-scatter.20
  317.8 27.2 all-gather.16
  346.8 27.4 all-gather.24
  392.1 43.3 reduce-scatter.24
  438.4 26.4 reduce-scatter.18
  468.0 26.5 all-gather.18
  496.3 27.4 all-gather.20
  561.4 43.3 reduce-scatter.22
  607.0 43.1 reduce-scatter.26
  653.0 27.1 reduce-scatter.14
  683.5 69.9 reduce-scatter.28
  757.4 156.8 reduce-scatter.32
  918.6 51.3 reduce-scatter.30
  973.9 92.3 reduce-scatter.34
where the time goes:
time: 1080 us; the launch traced here: 1070 us
  waiting for transfers between devices  723 us (67%)
  matrix products  156 us (14%)
  local copies, waits for them, and re-layouts  73.9 us (7%)
  other arithmetic  61.7 us (6%)
  blocking collectives  41.1 us (4%)
  between operations  16.1 us (1%)
    reduce_scatter x1, waiting for transfers between devices, local(): lax.psum_scatter(totals[1], 'wide', scatter_dimension=0, tiled=True)  157 us
    reduce_scatter x1, waiting for transfers between devices, local(): lax.psum_scatter(totals[3], 'wide', scatter_dimension=1, tiled=True)  96.3 us
    reduce_scatter x2, waiting for transfers between devices, local(): lax.psum_scatter(row_back_product(d_both, w_both), 'narrow', scatter_dime...  78.7 us
    reduce_scatter x2, waiting for transfers between devices, local(): lax.psum_scatter(row_product(attn_mix, w_out), 'narrow', scatter_dimensio...  77.3 us
    reduce_scatter x1, waiting for transfers between devices, local(): lax.psum_scatter(totals[0], 'wide', scatter_dimension=0, tiled=True)  56.1 us
    reduce_scatter x1, waiting for transfers between devices, local(): lax.psum_scatter(totals[2], 'wide', scatter_dimension=1, tiled=True)  51.9 us
    dot_general x8, matrix products, contract_rows(): lax.dot_general(left_side, right_side, (((0,), (0,)), ((), ())), preferre...  48.3 us
    dot_general x8, matrix products, contract_cols(): lax.dot_general(left_side, right_side, (((1,), (1,)), ((), ())), preferre...  48.1 us
  transfers between devices with their start and end apart: 20, of which 18 were waited for; matrix products, arithmetic and copies ran while one was open for 16% of the time, Pallas kernels for 0%

commit v1 on v0

--- a/solution.py
+++ b/solution.py
@@ -118,7 +118,16 @@
         scale_one = rms_scale(rows_in)
         hat_one = rows_in * scale_one
         normed = (hat_one * attn_gain_f).astype(jnp.bfloat16)
-        normed_full = lax.all_gather(normed, "narrow", axis=0, tiled=True)
+        ring = [normed]
+        for hop in range(3):
+            ring.append(
+                lax.ppermute(ring[-1], "narrow", [(dev, (dev + 1) % 4) for dev in range(4)])
+            )
+        normed_full = jnp.roll(
+            jnp.concatenate(ring[::-1], axis=0),
+            (lax.axis_index("narrow") + 1) * ring[0].shape[0],
+            axis=0,
+        )
         projected = jnp.dot(normed_full, w_qkv, preferred_element_type=jnp.float32)
         query_raw = projected[:, :query_cols].reshape(seq_len, query_heads, head_dim)
         key_raw = projected[:, query_cols : query_cols + key_cols].reshape(

time: 1080 us -> 1050 us (0.972)
  waiting for transfers between devices: 723 us -> 705 us
    all_gather x2 -> x0, waiting for transfers between devices: 42.9 us -> none  [local(): normed_full = lax.all_gather(normed, 'narrow', axis=0, tiled=True)]
    ppermute x0 -> x6, waiting for transfers between devices: none -> 21.1 us  [local(): lax.ppermute(ring[-1], 'narrow', [(dev, (dev + 1) % 4) for dev in range(4)])]
    unnamed x217 -> x263, local copies, waits for them, and re-layouts: 27.1 us -> 25.9 us
  transfers between devices with their start and end apart: 20 -> 24, of which waited for: 18 -> 21; matrix products, arithmetic and copies ran while one was open for 16% -> 15% of each run, Pallas kernels for 0% -> 0%
where the time goes in v1:
time: 1050 us; the launch traced here: 1040 us
  waiting for transfers between devices  705 us (67%)
  matrix products  147 us (14%)
  local copies, waits for them, and re-layouts  68.5 us (7%)
  other arithmetic  57 us (5%)
  blocking collectives  41.1 us (4%)
  between operations  16.1 us (2%)
    reduce_scatter x1, waiting for transfers between devices, local(): lax.psum_scatter(totals[1], 'wide', scatter_dimension=0, tiled=True)  157 us
    reduce_scatter x1, waiting for transfers between devices, local(): lax.psum_scatter(totals[3], 'wide', scatter_dimension=1, tiled=True)  96.4 us
    reduce_scatter x2, waiting for transfers between devices, local(): lax.psum_scatter(row_back_product(d_both, w_both), 'narrow', scatter_dime...  78.6 us
    reduce_scatter x2, waiting for transfers between devices, local(): lax.psum_scatter(row_product(attn_mix, w_out), 'narrow', scatter_dimensio...  78.1 us
    reduce_scatter x1, waiting for transfers between devices, local(): lax.psum_scatter(totals[0], 'wide', scatter_dimension=0, tiled=True)  56 us
    reduce_scatter x1, waiting for transfers between devices, local(): lax.psum_scatter(totals[2], 'wide', scatter_dimension=1, tiled=True)  51.7 us
    dot_general x8, matrix products, contract_rows(): lax.dot_general(left_side, right_side, (((0,), (0,)), ((), ())), preferre...  48.4 us
    dot_general x8, matrix products, contract_cols(): lax.dot_general(left_side, right_side, (((1,), (1,)), ((), ())), preferre...  43.7 us
  transfers between devices with their start and end apart: 24, of which 21 were waited for; matrix products, arithmetic and copies ran while one was open for 15% of the time, Pallas kernels for 0%

profile of v1, /device:TPU:0, one launch (start us, length us, event | category | flops | bytes accessed | tf_op | source)
XLA Modules:
  0.0 1042.0 jit_solution(16921173284426232183)
XLA Ops:
  90.4 32.5 %reduce-scatter.13.cloned.1.call-done = f32[64,2048]{1,0:T(8,128)} async-done(((f32[256,2048]{1,0:T(8,128)}), f32[64,2048]{1,0:T(8,128)}) %reduce-scatter.13.cloned.1.call-update) | async-done | bytes 524304 | tf_op jit(solution)/shard_map/reduce_scatter | solution.py:158
  122.9 45.6 %reduce-scatter.17.cloned.1.call-done = f32[64,2048]{1,0:T(8,128)} async-done(((f32[256,2048]{1,0:T(8,128)}), f32[64,2048]{1,0:T(8,128)}) %reduce-scatter.17.cloned.1.call-update) | async-done | bytes 524304 | tf_op jit(solution)/shard_map/reduce_scatter | solution.py:158
  187.6 13.0 %all-gather.9.cloned.1.call-done = bf16[256,2048]{1,0:T(8,128)(2,1)} async-done(((bf16[64,2048]{1,0:T(8,128)(2,1)}), bf16[256,2048]{1,0:T(8,128)(2,1)}) %all-gather.9.cloned.1.call-update) | async-done | bytes 1048592 | tf_op jit(solution)/shard_map/all_gather | solution.py:165
  200.5 9.9 fusion.126
  210.5 18.9 %all-gather.17.cloned.1.call-done = bf16[1,1,256,2048]{3,2,1,0:T(8,128)(2,1)} async-done(((bf16[1,1,64,2048]{3,2,1,0:T(8,128)(2,1)}), bf16[1,1,256,2048]{3,2,1,0:T(8,128)(2,1)}) %all-gather.17.cloned.1.call-update) | async-done | bytes 1048592 | tf_op jit(solution)/shard_map/all_gather | solution.py:180
  237.8 9.3 fusion.35
  248.3 42.3 %reduce-scatter.21.cloned.1.call-done = f32[64,2048]{1,0:T(8,128)} async-done(((f32[256,2048]{1,0:T(8,128)}), f32[64,2048]{1,0:T(8,128)}) %reduce-scatter.21.cloned.1.call-update) | async-done | bytes 524304 | tf_op jit(solution)/shard_map/reduce_scatter | solution.py:187
  294.5 26.4 %all-gather.11.cloned.1.call-done = bf16[256,2048]{1,0:T(8,128)(2,1)} async-done(((bf16[64,2048]{1,0:T(8,128)(2,1)}), bf16[256,2048]{1,0:T(8,128)(2,1)}) %all-gather.11.cloned.1.call-update) | async-done | bytes 1048592 | tf_op jit(solution)/shard_map/all_gather | solution.py:165
  321.0 9.9 fusion.129
  330.9 19.2 %all-gather.19.cloned.1.call-done = bf16[1,1,256,2048]{3,2,1,0:T(8,128)(2,1)} async-done(((bf16[1,1,64,2048]{3,2,1,0:T(8,128)(2,1)}), bf16[1,1,256,2048]{3,2,1,0:T(8,128)(2,1)}) %all-gather.19.cloned.1.call-update) | async-done | bytes 1048592 | tf_op jit(solution)/shard_map/all_gather | solution.py:180
  350.1 7.3 multiply_convert_fusion.1
  358.5 9.4 fusion.33
  375.0 36.3 %reduce-scatter.25.cloned.1.call-done = f32[64,2048]{1,0:T(8,128)} async-done(((f32[256,2048]{1,0:T(8,128)}), f32[64,2048]{1,0:T(8,128)}) %reduce-scatter.25.cloned.1.call-update) | async-done | bytes 524304 | tf_op jit(solution)/shard_map/reduce_scatter | solution.py:187
  413.8 26.9 %reduce-scatter.19.cloned.1.call-done = bf16[64,2048]{1,0:T(8,128)(2,1)} async-done(((bf16[256,2048]{1,0:T(8,128)(2,1)}), bf16[64,2048]{1,0:T(8,128)(2,1)}) %reduce-scatter.19.cloned.1.call-update) | async-done | bytes 262160 | tf_op jit(solution)/shard_map/reduce_scatter | solution.py:172
  449.3 21.1 %all-gather.13.cloned.1.call-done = bf16[256,2048]{1,0:T(8,128)(2,1)} async-done(((bf16[64,2048]{1,0:T(8,128)(2,1)}), bf16[256,2048]{1,0:T(8,128)(2,1)}) %all-gather.13.cloned.1.call-update) | async-done | bytes 1048592 | tf_op jit(solution)/shard_map/all_gather | solution.py:195
  480.2 19.3 %all-gather.15.cloned.1.call-done = bf16[256,2048]{1,0:T(8,128)(2,1)} async-done(((bf16[64,2048]{1,0:T(8,128)(2,1)}), bf16[256,2048]{1,0:T(8,128)(2,1)}) %all-gather.15.cloned.1.call-update) | async-done | bytes 1048592 | tf_op jit(solution)/shard_map/all_gather | solution.py:195
  554.5 11.6 %fusion.34 = f32[2048,3072]{1,0:T(8,128)} fusion(bf16[256,2048]{1,0:T(8,128)(2,1)S(1)} %copy-done.49, bf16[256,1536]{1,0:T(8,128)(2,1)} %copy-done.82, bf16[256,1536]{1,0:T(8,128)(2,1)} %copy-done.81), kind=kOutput, calls=%fused_computation.92 | convolution fusion | flops 3224371200 | bytes 27787264 | tf_op jit(solution)/shard_map/dot_general | solution.py:51
  566.1 17.1 %convolution_add_fusion = f32[2048,3072]{1,0:T(8,128)} fusion(f32[2048,3072]{1,0:T(8,128)} %fusion.34, bf16[256,2048]{1,0:T(8,128)(2,1)S(1)} %copy-done.46, bf16[256,1536]{1,0:T(8,128)(2,1)} %copy-done.79, bf16[256,1536]{1,0:T(8,128)(2,1)S(1)} %copy-done.78), kind=kOutput, calls=%fused_computation | convolution fusion | flops 3230662656 | bytes 52953088 | tf_op jit(solution)/shard_map/dot_general | solution.py:51
  599.4 19.5 %reduce-scatter.27.cloned.1.call-done = f32[64,2048]{1,0:T(8,128)} async-done(((f32[256,2048]{1,0:T(8,128)}), f32[64,2048]{1,0:T(8,128)}) %reduce-scatter.27.cloned.1.call-update) | async-done | bytes 524304 | tf_op jit(solution)/shard_map/reduce_scatter | solution.py:229
  620.6 41.1 %all-reduce = (f32[2048]{0:T(1024)}, f32[128]{0:T(128)}, f32[128]{0:T(128)}, f32[2048]{0:T(1024)}) all-reduce(f32[2048]{0:T(1024)S(1)} %add.239, f32[128]{0:T(128)S(1)} %add.241, f32[128]{0:T(128)S(1)} %add.242, f32[2048]{0:T(1024)S(1)} %add.244), channel_id=1, replica_groups=mesh['wide'=8,'narrow'=4] {'wide','narrow'}, use_global_device_ids=true, to_apply=%region_38.40 | all-reduce | flops 4352 | bytes 34816 | tf_op jit(solution)/shard_map/psum | solution.py:250
  666.2 56.0 %reduce-scatter.29.cloned.1.call-done = f32[256,1024]{1,0:T(8,128)} async-done(((f32[2048,1024]{1,0:T(8,128)}), f32[256,1024]{1,0:T(8,128)}) %reduce-scatter.29.cloned.1.call-update) | async-done | bytes 1048592 | tf_op jit(solution)/shard_map/reduce_scatter | solution.py:245
  726.1 157.0 %reduce-scatter.33.cloned.1.call-done = f32[256,3072]{1,0:T(8,128)} async-done(((f32[2048,3072]{1,0:T(8,128)}), f32[256,3072]{1,0:T(8,128)}) %reduce-scatter.33.cloned.1.call-update) | async-done | bytes 3145744 | tf_op jit(solution)/shard_map/reduce_scatter | solution.py:246
  886.8 51.7 %reduce-scatter.31.cloned.1.call-done = f32[512,256]{1,0:T(8,128)} async-done(((f32[512,2048]{1,0:T(8,128)}), f32[512,256]{1,0:T(8,128)}) %reduce-scatter.31.cloned.1.call-update) | async-done | bytes 524304 | tf_op jit(solution)/shard_map/reduce_scatter | solution.py:247
  938.6 96.4 %reduce-scatter.35.cloned.1.call-done = f32[1536,256]{1,0:T(8,128)} async-done(((f32[1536,2048]{1,0:T(8,128)}), f32[1536,256]{1,0:T(8,128)}) %reduce-scatter.35.cloned.1.call-update) | async-done | bytes 1572880 | tf_op jit(solution)/shard_map/reduce_scatter | solution.py:248
  (464 shorter events, 228.1 us)
Async XLA Ops:
  7.2 115.7 %reduce-scatter.13.cloned.1.call-start = ((), (), s32[]{:S(2)}) async-start(), calls=%async_computation.12 | async-start | bytes 2621440 | tf_op jit(solution)/shard_map/reduce_scatter | solution.py:158
  10.6 12.2 %collective-permute-start = (bf16[64,2048]{1,0:T(8,128)(2,1)S(1)}, bf16[64,2048]{1,0:T(8,128)(2,1)S(1)}, u32[]{:S(2)}, u32[]{:S(2)}) collective-permute-start(bf16[64,2048]{1,0:T(8,128)(2,1)S(1)} %get-tuple-element.137), channel_id=1, source_target_pairs={{0,1},{1,2},{2,3},{3,0},{4,5},{5,6},{6,7},{7,4},{8,9},{9,10},{10,1... | collective-permute-start | bytes 786440 | tf_op jit(solution)/shard_map/ppermute | solution.py:124
  13.7 14.8 %collective-permute-start.3 = (bf16[64,2048]{1,0:T(8,128)(2,1)S(1)}, bf16[64,2048]{1,0:T(8,128)(2,1)S(1)}, u32[]{:S(2)}, u32[]{:S(2)}) collective-permute-start(bf16[64,2048]{1,0:T(8,128)(2,1)S(1)} %get-tuple-element.138), channel_id=1, source_target_pairs={{0,1},{1,2},{2,3},{3,0},{4,5},{5,6},{6,7},{7,4},{8,9},{9,10},{10,1... | collective-permute-start | bytes 786440 | tf_op jit(solution)/shard_map/ppermute | solution.py:124
  22.8 11.3 %collective-permute-start.1 = (bf16[64,2048]{1,0:T(8,128)(2,1)S(1)}, bf16[64,2048]{1,0:T(8,128)(2,1)}, u32[]{:S(2)}, u32[]{:S(2)}) collective-permute-start(bf16[64,2048]{1,0:T(8,128)(2,1)S(1)} %collective-permute-done), channel_id=1, source_target_pairs={{0,1},{1,2},{2,3},{3,0},{4,5},{5,6},{6,7},{7,4},{8,9},{9,10},{10,1... | collective-permute-start | bytes 786440 | tf_op jit(solution)/shard_map/ppermute | solution.py:124
  28.4 11.3 %collective-permute-start.4 = (bf16[64,2048]{1,0:T(8,128)(2,1)S(1)}, bf16[64,2048]{1,0:T(8,128)(2,1)}, u32[]{:S(2)}, u32[]{:S(2)}) collective-permute-start(bf16[64,2048]{1,0:T(8,128)(2,1)S(1)} %collective-permute-done.3), channel_id=1, source_target_pairs={{0,1},{1,2},{2,3},{3,0},{4,5},{5,6},{6,7},{7,4},{8,9},{9,10},{10,1... | collective-permute-start | bytes 786440 | tf_op jit(solution)/shard_map/ppermute | solution.py:124
  34.1 11.4 %collective-permute-start.2 = (bf16[64,2048]{1,0:T(8,128)(2,1)}, bf16[64,2048]{1,0:T(8,128)(2,1)}, u32[]{:S(2)}, u32[]{:S(2)}) collective-permute-start(bf16[64,2048]{1,0:T(8,128)(2,1)} %collective-permute-done.1), channel_id=1, source_target_pairs={{0,1},{1,2},{2,3},{3,0},{4,5},{5,6},{6,7},{7,4},{8,9},{9,10},{10,1... | collective-permute-start | bytes 786440 | tf_op jit(solution)/shard_map/ppermute | solution.py:124
  39.8 14.4 %collective-permute-start.5 = (bf16[64,2048]{1,0:T(8,128)(2,1)}, bf16[64,2048]{1,0:T(8,128)(2,1)S(1)}, u32[]{:S(2)}, u32[]{:S(2)}) collective-permute-start(bf16[64,2048]{1,0:T(8,128)(2,1)} %collective-permute-done.4), channel_id=1, source_target_pairs={{0,1},{1,2},{2,3},{3,0},{4,5},{5,6},{6,7},{7,4},{8,9},{9,10},{10,1... | collective-permute-start | bytes 786440 | tf_op jit(solution)/shard_map/ppermute | solution.py:124
  79.3 89.2 %reduce-scatter.17.cloned.1.call-start = ((), (), s32[]{:S(2)}) async-start(), calls=%async_computation.15 | async-start | bytes 2621440 | tf_op jit(solution)/shard_map/reduce_scatter | solution.py:158
  89.7 110.8 %all-gather.9.cloned.1.call-start = ((), (), s32[]{:S(2)}) async-start(), calls=%async_computation.13 | async-start | bytes 1310720 | tf_op jit(solution)/shard_map/all_gather | solution.py:165
  173.1 56.3 %all-gather.17.cloned.1.call-start = ((), (), s32[]{:S(2)}) async-start(), calls=%async_computation.28 | async-start | bytes 1310720 | tf_op jit(solution)/shard_map/all_gather | solution.py:180
  175.1 115.6 %reduce-scatter.21.cloned.1.call-start = ((), (), s32[]{:S(2)}) async-start(), calls=%async_computation.18 | async-start | bytes 2621440 | tf_op jit(solution)/shard_map/reduce_scatter | solution.py:187
  247.1 73.8 %all-gather.11.cloned.1.call-start = ((), (), s32[]{:S(2)}) async-start(), calls=%async_computation.16 | async-start | bytes 1310720 | tf_op jit(solution)/shard_map/all_gather | solution.py:165
  293.6 56.5 %all-gather.19.cloned.1.call-start = ((), (), s32[]{:S(2)}) async-start(), calls=%async_computation.29 | async-start | bytes 1310720 | tf_op jit(solution)/shard_map/all_gather | solution.py:180
  294.3 117.0 %reduce-scatter.25.cloned.1.call-start = ((), (), s32[]{:S(2)}) async-start(), calls=%async_computation.21 | async-start | bytes 2621440 | tf_op jit(solution)/shard_map/reduce_scatter | solution.py:187
  367.8 72.9 %reduce-scatter.19.cloned.1.call-start = ((), (), s32[]{:S(2)}) async-start(), calls=%async_computation.17 | async-start | bytes 1310720 | tf_op jit(solution)/shard_map/reduce_scatter | solution.py:172
  373.7 96.7 %all-gather.13.cloned.1.call-start = ((), (), s32[]{:S(2)}) async-start(), calls=%async_computation.19 | async-start | bytes 1310720 | tf_op jit(solution)/shard_map/all_gather | solution.py:195
  443.7 55.9 %all-gather.15.cloned.1.call-start = ((), (), s32[]{:S(2)}) async-start(), calls=%async_computation.22 | async-start | bytes 1310720 | tf_op jit(solution)/shard_map/all_gather | solution.py:195
  444.4 155.0 %reduce-scatter.23.cloned.1.call-start = ((), (), s32[]{:S(2)}) async-start(), calls=%async_computation.20 | async-start | bytes 2621440 | tf_op jit(solution)/shard_map/reduce_scatter | solution.py:229
  529.9 89.0 %reduce-scatter.27.cloned.1.call-start = ((), (), s32[]{:S(2)}) async-start(), calls=%async_computation.23 | async-start | bytes 2621440 | tf_op jit(solution)/shard_map/reduce_scatter | solution.py:229
  539.4 122.4 %reduce-scatter.15.cloned.1.call-start = ((), (), s32[]{:S(2)}) async-start(), calls=%async_computation.14 | async-start | bytes 1310720 | tf_op jit(solution)/shard_map/reduce_scatter | solution.py:172
  546.2 176.0 %reduce-scatter.29.cloned.1.call-start = ((), (), s32[]{:S(2)}) async-start(), calls=%async_computation.24 | async-start | bytes 9437184 | tf_op jit(solution)/shard_map/reduce_scatter | solution.py:245
  553.3 329.8 %reduce-scatter.33.cloned.1.call-start = ((), (), s32[]{:S(2)}) async-start(), calls=%async_computation.26 | async-start | bytes 28311552 | tf_op jit(solution)/shard_map/reduce_scatter | solution.py:246
  583.2 355.4 %reduce-scatter.31.cloned.1.call-start = ((), (), s32[]{:S(2)}) async-start(), calls=%async_computation.25 | async-start | bytes 4718592 | tf_op jit(solution)/shard_map/reduce_scatter | solution.py:247
  588.0 446.9 %reduce-scatter.35.cloned.1.call-start = ((), (), s32[]{:S(2)}) async-start(), calls=%async_computation.27 | async-start | bytes 14155776 | tf_op jit(solution)/shard_map/reduce_scatter | solution.py:248
  (127 other events, 1579.6 us)
Sparse Core Ops, SparseCore 0:
  79.4 43.4 reduce-scatter.12
  125.3 43.1 reduce-scatter.16
  173.2 27.2 all-gather.8
  201.9 27.4 all-gather.16
  247.2 43.3 reduce-scatter.20
  293.7 27.2 all-gather.10
  322.6 27.4 all-gather.18
  368.0 43.3 reduce-scatter.24
  414.2 26.4 reduce-scatter.18
  443.8 26.5 all-gather.12
  472.1 27.4 all-gather.14
  530.0 43.3 reduce-scatter.22
  575.7 43.1 reduce-scatter.26
  621.7 27.1 reduce-scatter.14
  652.3 69.9 reduce-scatter.28
  726.2 156.8 reduce-scatter.32
  887.2 51.2 reduce-scatter.30
  942.5 92.3 reduce-scatter.34
